TPU v7x, 32 devices: a whole 2x2x4 slice. The times are simulated.
32 devices in a mesh: rows: 8 (over y, x, core), feat: 4 (over z).
Axes of the slice: x: 2, y: 2, z: 4, core: 2. Of those that a mesh axis runs over, the one named last changes fastest.
Arguments:
- queries: bfloat16 [49152, 4096], P('rows', 'feat'), may hold values from -6 to 6
- projection: bfloat16 [4096, 128], P('feat'), may hold values from -0.09375 to 0.09375
- models: float32 [64, 128], replicated, may hold values from -0.5 to 0.5
- first: int32 [49152], P('rows'), may hold values from 0 to 63
- second: int32 [49152], P('rows'), may hold values from 0 to 63
- wins: int32 [49152], P('rows'), may hold values 0 or 1
Outputs:
- update_proj: float32 [4096, 128], P('feat')
- update_models: float32 [64, 128], replicated
- loss: float32 [], replicated
All inputs are finite; a program needn't handle non-finite values. No bound on the sum of `wins` on one device may be relied on, other than what follows from the above.
Results may differ from a plain program's by a relative error of at most 0.00045.
The roundings to bfloat16 on the way count: a program that leaves them out, or rounds other values in their place, can miss the bound.
Values may be sent and summed in bfloat16 or wider, within the bound.
A program may use at most 64 MiB of HBM per device.

v0:
```python
import jax
import jax.numpy as jnp
from jax import lax
from jax.sharding import PartitionSpec as P

D = 4096
R = 128
NM = 64


def pair_gap(models, first, second):
    return jnp.take(models, first, axis=0) - jnp.take(models, second, axis=0)


def pick_table(models, first, second):
    labels = jnp.arange(models.shape[0], dtype=jnp.int32)[:, None]
    return (labels == first[None, :]).astype(jnp.float32) - (labels == second[None, :]).astype(
        jnp.float32
    )


def body(queries, projection, models, first, second, wins):
    local_rows = queries.shape[0]
    total_rows = float(local_rows * lax.axis_size("rows"))
    partial_value = jnp.dot(queries, projection, preferred_element_type=jnp.float32)
    gap = pair_gap(models, first, second)
    margin = lax.psum(jnp.sum(partial_value * gap, axis=-1), "feat")
    sign = 2.0 * wins.astype(jnp.float32) - 1.0
    loss_part = jnp.sum(jax.nn.softplus(-sign * margin)) / total_rows
    coef = -sign * jax.nn.sigmoid(-sign * margin) / total_rows
    back = (coef[:, None] * gap).astype(jnp.bfloat16)
    pick = pick_table(models, first, second)
    model_part = jnp.dot(pick, coef[:, None] * partial_value, precision=lax.Precision.HIGHEST)
    feat_count = float(lax.axis_size("feat"))
    grad_models, loss = lax.psum((model_part, loss_part / feat_count), ("rows", "feat"))
    model_square = jnp.sum(grad_models * grad_models)
    entries = jnp.sqrt(jnp.float32(D * R + NM * R))
    grad_local = jnp.dot(queries.T, back, preferred_element_type=jnp.float32)
    grad_proj = lax.psum(grad_local, "rows")
    square = lax.psum(jnp.sum(grad_proj * grad_proj), "feat")
    scale = entries / (jnp.sqrt(square + model_square) + 1e-06)
    update_proj = scale * grad_proj
    return (update_proj, scale * grad_models, loss)


def solution(mesh):
    in_specs = (P("rows", "feat"), P("feat", None), P(), P("rows"), P("rows"), P("rows"))
    out_specs = (P("feat", None), P(), P())
    return jax.shard_map(body, mesh=mesh, in_specs=in_specs, out_specs=out_specs, check_vma=False)
```

profile of v0, /device:TPU:0, one launch (start us, length us, event | category | flops | bytes accessed | tf_op | source)
XLA Modules:
  0.0 177.5 jit_solution(17190203566094224995)
XLA Ops:
  7.2 0.0 copy-start
  7.2 0.0 copy-start.1
  7.2 0.0 all-reduce.3.cloned.1.call-start
  7.2 0.7 fusion.14
  8.0 0.8 compare_and_fusion
  8.8 0.7 fusion.13
  9.5 0.0 copy-done.1
  9.5 20.9 %gather_fusion.1 = f32[6144,128]{1,0:T(8,128)} fusion(f32[64,128]{1,0:T(8,128)S(1)} %copy-done.1, s32[6144]{0:T(1024)S(1)} %fusion.14), kind=kCustom, calls=%fused_computation.1.clone | custom fusion | bytes 6316032 | tf_op jit(solution)/shard_map/jit(_take)/gather | solution.py:12
  30.4 2.4 %copy.10 = f32[6144,128]{0,1:T(8,128)S(1)} copy(f32[6144,128]{1,0:T(8,128)} %gather_fusion.1) | data formatting | bytes 6291456 | tf_op jit(solution)/shard_map/jit(_take)/gather | solution.py:12
  32.8 20.9 %gather_fusion = f32[6144,128]{1,0:T(8,128)} fusion(f32[64,128]{1,0:T(8,128)S(1)} %copy-done.1, s32[6144]{0:T(1024)S(1)} %fusion.13), kind=kCustom, calls=%fused_computation.clone | custom fusion | bytes 6316032 | tf_op jit(solution)/shard_map/jit(_take)/gather | solution.py:12
  53.7 3.5 %copy.9 = f32[6144,128]{0,1:T(8,128)} copy(f32[6144,128]{1,0:T(8,128)} %gather_fusion) | data formatting | bytes 6291456 | tf_op jit(solution)/shard_map/jit(_take)/gather | solution.py:12
  57.2 0.0 copy-done
  57.2 0.0 copy-start.4
  57.2 11.7 %multiply_reduce_fusion = (f32[6144]{0:T(1024)S(1)}, f32[6144,128]{0,1:T(8,128)}) fusion(f32[6144,128]{0,1:T(8,128)S(1)} %copy.10, pred[6144]{0:T(1024)(128)(4,1)S(1)} %get-tuple-element.13, f32[6144,128]{0,1:T(8,128)} %copy.9, pred[6144]{0:T(1024)(128)(4,1)S(1)} %get-tuple-element.14, bf16[6144,1024]{1,0:T(8,128)(2,1)} %param.8, ...), kind=kOutput, calls=%fused_computation.6 | convolution fusion | flops 1614538752 | bytes 22319104 | tf_op jit(solution)/shard_map/dot_general | solution.py:25
  68.9 20.8 %psum.35 = f32[6144]{0:T(1024)S(1)} all-reduce(f32[6144]{0:T(1024)S(1)} %get-tuple-element.11), channel_id=1, replica_groups=mesh['rows'=8,'feat'=4] {'feat'}, use_global_device_ids=true, to_apply=%region_1.3 | all-reduce | flops 6144 | bytes 49152 | tf_op jit(solution)/shard_map/psum | solution.py:27
  89.6 0.0 copy-done.4
  89.6 0.6 fusion.11
  90.3 0.0 copy-start.2
  90.3 0.0 copy-start.3
  90.3 8.3 %fusion.8 = f32[1024,128]{0,1:T(8,128)} fusion(bf16[6144,1024]{1,0:T(8,128)(2,1)} %param.8, f32[6144]{0:T(1024)S(1)} %get-tuple-element.10, f32[6144,128]{0,1:T(8,128)S(1)} %copy.10, f32[6144,128]{0,1:T(8,128)} %copy.9, pred[6144]{0:T(1024)(128)(4,1)S(1)} %get-tuple-element.13, pred[6144]{0:T(1024)(128)(4,1)S(1)} %get-tuple-element.14), kind=kOutput, calls=%fused_computation.15 | convolution fusion | flops 1614544896 | bytes 19435520 | tf_op jit(solution)/shard_map/dot_general | solution.py:38
  98.6 0.0 all-reduce.3.cloned.1.call-update
  99.2 0.0 copy-done.2
  99.2 0.0 copy-done.3
  99.3 5.2 %fusion = f32[64,128]{1,0:T(8,128)S(1)} fusion(f32[6144,128]{0,1:T(8,128)} %get-tuple-element.12, f32[6144]{0:T(1024)S(1)} %get-tuple-element.10, s32[6144]{0:T(1024)S(1)} %copy-done.2, s32[6144]{0:T(1024)S(1)} %copy-done.3), kind=kOutput, calls=%fused_computation.3 | convolution fusion | flops 606732288 | bytes 3252224 | tf_op jit(solution)/shard_map/dot_general | solution.py:33
  104.4 38.9 %all-reduce = (f32[64,128]{1,0:T(8,128)S(1)}, f32[]{:T(128)}) all-reduce(f32[64,128]{1,0:T(8,128)S(1)} %fusion, f32[]{:T(128)S(6)} %div.20), channel_id=1, replica_groups=mesh['rows'=8,'feat'=4] {'rows','feat'}, use_global_device_ids=true, to_apply=%region_5.7 | all-reduce | flops 8193 | bytes 65544 | tf_op jit(solution)/shard_map/psum | solution.py:35
  143.3 8.6 %all-reduce.3.cloned.1.call-done = f32[1024,128]{0,1:T(8,128)} async-done(((f32[1024,128]{0,1:T(8,128)}), f32[1024,128]{0,1:T(8,128)}) %all-reduce.3.cloned.1.call-update) | async-done | bytes 524304 | tf_op jit(solution)/shard_map/psum | solution.py:39
  151.9 1.8 %multiply_reduce_fusion.1 = f32[]{:T(128)} fusion(f32[1024,128]{0,1:T(8,128)} %all-reduce.3.cloned.1.call-done), kind=kLoop, calls=%fused_computation.18 | loop fusion | flops 262143 | bytes 524292 | tf_op jit(solution)/shard_map/reduce_sum | solution.py:40
  153.7 0.6 multiply_reduce_fusion.2
  154.3 12.2 %psum.37 = f32[]{:T(128)} all-reduce(f32[]{:T(128)} %multiply_reduce_fusion.1), channel_id=1, replica_groups=mesh['rows'=8,'feat'=4] {'feat'}, use_global_device_ids=true, to_apply=%region_4.6 | all-reduce | flops 1 | bytes 8 | tf_op jit(solution)/shard_map/psum | solution.py:40
  168.0 0.6 broadcast_multiply_fusion.1
  168.6 1.1 broadcast_multiply_fusion
  169.7 1.0 copy.11
Async XLA Ops:
  7.2 50.0 %copy-start = (bf16[1024,128]{1,0:T(8,128)(2,1)S(1)}, bf16[1024,128]{1,0:T(8,128)(2,1)}, u32[]{:S(2)}) copy-start(bf16[1024,128]{1,0:T(8,128)(2,1)} %param.9) | copy-start | bytes 786436
  7.2 2.3 %copy-start.1 = (f32[64,128]{1,0:T(8,128)S(1)}, f32[64,128]{1,0:T(8,128)}, u32[]{:S(2)}) copy-start(f32[64,128]{1,0:T(8,128)} %param.10) | copy-start | bytes 98308
  7.2 144.8 %all-reduce.3.cloned.1.call-start = ((), (), s32[]{:S(2)}) async-start(), calls=%async_computation | async-start | bytes 1048576 | tf_op jit(solution)/shard_map/psum | solution.py:39
  57.2 32.4 %copy-start.4 = (s32[6144]{0:T(1024)S(1)}, s32[6144]{0:T(1024)}, u32[]{:S(2)}) copy-start(s32[6144]{0:T(1024)} %param.13) | copy-start | bytes 73732
  90.3 9.0 %copy-start.2 = (s32[6144]{0:T(1024)S(1)}, s32[6144]{0:T(1024)}, u32[]{:S(2)}) copy-start(s32[6144]{0:T(1024)} %param.12) | copy-start | bytes 73732
  90.3 9.0 %copy-start.3 = (s32[6144]{0:T(1024)S(1)}, s32[6144]{0:T(1024)}, u32[]{:S(2)}) copy-start(s32[6144]{0:T(1024)} %param.11) | copy-start | bytes 73732
Sparse Core Ops, SparseCore 0:
  98.7 53.1 all-reduce.2
where the time goes:
time: 178 us
  blocking collectives  71.9 us (40%)
  local copies, waits for them, and re-layouts  48.7 us (27%)
  matrix products  25.1 us (14%)
  between operations  16.1 us (9%)
  waiting for transfers between devices  8.62 us (5%)
  other arithmetic  6.98 us (4%)
    gather x4, local copies, waits for them, and re-layouts, pair_gap(): return jnp.take(models, first, axis=0) - jnp.take(models, second, axis=0)  47.7 us
    psum x1, blocking collectives, body(): lax.psum((model_part, loss_part / feat_count), ('rows', 'feat'))  38.9 us
    psum x1, blocking collectives, body(): margin = lax.psum(jnp.sum(partial_value * gap, axis=-1), 'feat')  20.8 us
    psum x1, blocking collectives, body(): square = lax.psum(jnp.sum(grad_proj * grad_proj), 'feat')  12.2 us
    dot_general x1, matrix products, body(): jnp.dot(queries, projection, preferred_element_type=jnp.float32)  11.7 us
    psum x1, waiting for transfers between devices, body(): grad_proj = lax.psum(grad_local, 'rows')  8.61 us
    dot_general x1, matrix products, body(): grad_local = jnp.dot(queries.T, back, preferred_element_type=jnp.float32)  8.29 us
    dot_general x1, matrix products, body(): jnp.dot(pick, coef[:, None] * partial_value, precision=lax.Precision.HIGH...  5.18 us
  transfers between devices with their start and end apart: 1, of which 1 were waited for; matrix products, arithmetic and copies ran while one was open for 3% of the time, Pallas kernels for 0%

commit v1 on v0

--- a/solution.py
+++ b/solution.py
@@ -6,6 +6,11 @@
 D = 4096
 R = 128
 NM = 64
+
+
+def axis_by_axis(value, one, other):
+    inner = lax.psum(value, one)
+    return lax.psum(inner, other)
 
 
 def pair_gap(models, first, second):
@@ -32,7 +37,7 @@
     pick = pick_table(models, first, second)
     model_part = jnp.dot(pick, coef[:, None] * partial_value, precision=lax.Precision.HIGHEST)
     feat_count = float(lax.axis_size("feat"))
-    grad_models, loss = lax.psum((model_part, loss_part / feat_count), ("rows", "feat"))
+    grad_models, loss = axis_by_axis((model_part, loss_part / feat_count), "rows", "feat")
     model_square = jnp.sum(grad_models * grad_models)
     entries = jnp.sqrt(jnp.float32(D * R + NM * R))
     grad_local = jnp.dot(queries.T, back, preferred_element_type=jnp.float32)

time: 178 us -> 186 us (1.045)
  waiting for transfers between devices: 8.62 us -> 24.1 us
  blocking collectives: 71.9 us -> 64.4 us
    psum x1, blocking collectives: 38.9 us -> 23.4 us  [axis_by_axis(): inner = lax.psum(value, one)]
    psum x1, waiting for transfers between devices: 8.61 us -> 24.1 us  [body(): grad_proj = lax.psum(grad_local, 'rows')]
    psum x1, blocking collectives: 12.2 us -> 20.3 us  [body(): square = lax.psum(jnp.sum(grad_proj * grad_proj), 'feat')]
where the time goes in v1:
time: 186 us; the launch traced here: 185 us
  blocking collectives  64.4 us (35%)
  local copies, waits for them, and re-layouts  48.7 us (26%)
  matrix products  25.1 us (13%)
  waiting for transfers between devices  24.1 us (13%)
  between operations  16.1 us (9%)
  other arithmetic  6.98 us (4%)
    gather x4, local copies, waits for them, and re-layouts, pair_gap(): return jnp.take(models, first, axis=0) - jnp.take(models, second, axis=0)  47.7 us
    psum x1, waiting for transfers between devices, body(): grad_proj = lax.psum(grad_local, 'rows')  24.1 us
    psum x1, blocking collectives, axis_by_axis(): inner = lax.psum(value, one)  23.4 us
    psum x1, blocking collectives, body(): margin = lax.psum(jnp.sum(partial_value * gap, axis=-1), 'feat')  20.8 us
    psum x1, blocking collectives, body(): square = lax.psum(jnp.sum(grad_proj * grad_proj), 'feat')  20.3 us
    dot_general x1, matrix products, body(): jnp.dot(queries, projection, preferred_element_type=jnp.float32)  11.7 us
    dot_general x1, matrix products, body(): grad_local = jnp.dot(queries.T, back, preferred_element_type=jnp.float32)  8.29 us
    dot_general x1, matrix products, body(): jnp.dot(pick, coef[:, None] * partial_value, precision=lax.Precision.HIGH...  5.18 us
  transfers between devices with their start and end apart: 1, of which 1 were waited for; matrix products, arithmetic and copies ran while one was open for 3% of the time, Pallas kernels for 0%

profile of v1, /device:TPU:0, one launch (start us, length us, event | category | flops | bytes accessed | tf_op | source)
XLA Modules:
  0.0 185.4 jit_solution(5378575236596506585)
XLA Ops:
  7.2 0.0 copy-start
  7.2 0.0 copy-start.1
  7.2 0.0 all-reduce.4.cloned.1.call-start
  7.2 0.7 fusion.14
  8.0 0.8 compare_and_fusion
  8.8 0.7 fusion.13
  9.5 0.0 copy-done.1
  9.5 20.9 %gather_fusion.1 = f32[6144,128]{1,0:T(8,128)} fusion(f32[64,128]{1,0:T(8,128)S(1)} %copy-done.1, s32[6144]{0:T(1024)S(1)} %fusion.14), kind=kCustom, calls=%fused_computation.1.clone | custom fusion | bytes 6316032 | tf_op jit(solution)/shard_map/jit(_take)/gather | solution.py:17
  30.4 2.4 %copy.10 = f32[6144,128]{0,1:T(8,128)S(1)} copy(f32[6144,128]{1,0:T(8,128)} %gather_fusion.1) | data formatting | bytes 6291456 | tf_op jit(solution)/shard_map/jit(_take)/gather | solution.py:17
  32.8 20.9 %gather_fusion = f32[6144,128]{1,0:T(8,128)} fusion(f32[64,128]{1,0:T(8,128)S(1)} %copy-done.1, s32[6144]{0:T(1024)S(1)} %fusion.13), kind=kCustom, calls=%fused_computation.clone | custom fusion | bytes 6316032 | tf_op jit(solution)/shard_map/jit(_take)/gather | solution.py:17
  53.7 3.5 %copy.9 = f32[6144,128]{0,1:T(8,128)} copy(f32[6144,128]{1,0:T(8,128)} %gather_fusion) | data formatting | bytes 6291456 | tf_op jit(solution)/shard_map/jit(_take)/gather | solution.py:17
  57.2 0.0 copy-done
  57.2 0.0 copy-start.4
  57.2 11.7 %multiply_reduce_fusion = (f32[6144]{0:T(1024)S(1)}, f32[6144,128]{0,1:T(8,128)}) fusion(f32[6144,128]{0,1:T(8,128)S(1)} %copy.10, pred[6144]{0:T(1024)(128)(4,1)S(1)} %get-tuple-element.16, f32[6144,128]{0,1:T(8,128)} %copy.9, pred[6144]{0:T(1024)(128)(4,1)S(1)} %get-tuple-element.17, bf16[6144,1024]{1,0:T(8,128)(2,1)} %param.8, ...), kind=kOutput, calls=%fused_computation.6 | convolution fusion | flops 1614538752 | bytes 22319104 | tf_op jit(solution)/shard_map/dot_general | solution.py:30
  68.9 20.8 %psum.49 = f32[6144]{0:T(1024)S(1)} all-reduce(f32[6144]{0:T(1024)S(1)} %get-tuple-element.14), channel_id=1, replica_groups=mesh['rows'=8,'feat'=4] {'feat'}, use_global_device_ids=true, to_apply=%region_1.3 | all-reduce | flops 6144 | bytes 49152 | tf_op jit(solution)/shard_map/psum | solution.py:32
  89.6 0.0 copy-done.4
  89.6 0.6 fusion.11
  90.3 0.0 copy-start.2
  90.3 0.0 copy-start.3
  90.3 8.3 %fusion.8 = f32[1024,128]{0,1:T(8,128)} fusion(bf16[6144,1024]{1,0:T(8,128)(2,1)} %param.8, f32[6144]{0:T(1024)S(1)} %get-tuple-element.13, f32[6144,128]{0,1:T(8,128)S(1)} %copy.10, f32[6144,128]{0,1:T(8,128)} %copy.9, pred[6144]{0:T(1024)(128)(4,1)S(1)} %get-tuple-element.16, pred[6144]{0:T(1024)(128)(4,1)S(1)} %get-tuple-element.17), kind=kOutput, calls=%fused_computation.15 | convolution fusion | flops 1614544896 | bytes 19435520 | tf_op jit(solution)/shard_map/dot_general | solution.py:43
  98.6 0.0 all-reduce.4.cloned.1.call-update
  99.2 0.0 copy-done.2
  99.2 0.0 copy-done.3
  99.3 5.2 %fusion = f32[64,128]{1,0:T(8,128)S(1)} fusion(f32[6144,128]{0,1:T(8,128)} %get-tuple-element.15, f32[6144]{0:T(1024)S(1)} %get-tuple-element.13, s32[6144]{0:T(1024)S(1)} %copy-done.2, s32[6144]{0:T(1024)S(1)} %copy-done.3), kind=kOutput, calls=%fused_computation.3 | convolution fusion | flops 606732288 | bytes 3252224 | tf_op jit(solution)/shard_map/dot_general | solution.py:38
  104.4 23.4 %all-reduce = (f32[64,128]{1,0:T(8,128)S(1)}, f32[]{:T(128)}) all-reduce(f32[64,128]{1,0:T(8,128)S(1)} %fusion, f32[]{:T(128)S(6)} %div.20), channel_id=1, replica_groups=mesh['rows'=8,'feat'=4] {'rows'}, use_global_device_ids=true, to_apply=%region_5.7 | all-reduce | flops 8193 | bytes 65544 | tf_op jit(solution)/shard_map/psum | solution.py:12
  127.8 24.1 %all-reduce.4.cloned.1.call-done = f32[1024,128]{0,1:T(8,128)} async-done(((f32[1024,128]{0,1:T(8,128)}), f32[1024,128]{0,1:T(8,128)}) %all-reduce.4.cloned.1.call-update) | async-done | bytes 524304 | tf_op jit(solution)/shard_map/psum | solution.py:44
  151.9 1.8 multiply_reduce_fusion.1
  153.7 20.3 %all-reduce.1 = (f32[]{:T(128)}, f32[64,128]{1,0:T(8,128)S(1)}, f32[]{:T(128)}) all-reduce(f32[]{:T(128)} %multiply_reduce_fusion.1, f32[64,128]{1,0:T(8,128)S(1)} %get-tuple-element.7, f32[]{:T(128)} %get-tuple-element.8), channel_id=1, replica_groups=mesh['rows'=8,'feat'=4] {'feat'}, use_global_device_ids=true, to_apply=%region_4.6 | all-reduce | flops 8194 | bytes 65552 | tf_op jit(solution)/shard_map/psum | solution.py:45
  173.9 0.6 multiply_reduce_fusion.2
  175.9 0.6 broadcast_multiply_fusion.1
  176.5 1.1 broadcast_multiply_fusion
  177.6 1.0 copy.11
Async XLA Ops:
  7.2 50.0 %copy-start = (bf16[1024,128]{1,0:T(8,128)(2,1)S(1)}, bf16[1024,128]{1,0:T(8,128)(2,1)}, u32[]{:S(2)}) copy-start(bf16[1024,128]{1,0:T(8,128)(2,1)} %param.9) | copy-start | bytes 786436
  7.2 2.3 %copy-start.1 = (f32[64,128]{1,0:T(8,128)S(1)}, f32[64,128]{1,0:T(8,128)}, u32[]{:S(2)}) copy-start(f32[64,128]{1,0:T(8,128)} %param.10) | copy-start | bytes 98308
  7.2 144.7 %all-reduce.4.cloned.1.call-start = ((), (), s32[]{:S(2)}) async-start(), calls=%async_computation | async-start | bytes 1048576 | tf_op jit(solution)/shard_map/psum | solution.py:44
  57.2 32.4 %copy-start.4 = (s32[6144]{0:T(1024)S(1)}, s32[6144]{0:T(1024)}, u32[]{:S(2)}) copy-start(s32[6144]{0:T(1024)} %param.13) | copy-start | bytes 73732
  90.3 9.0 %copy-start.2 = (s32[6144]{0:T(1024)S(1)}, s32[6144]{0:T(1024)}, u32[]{:S(2)}) copy-start(s32[6144]{0:T(1024)} %param.12) | copy-start | bytes 73732
  90.3 9.0 %copy-start.3 = (s32[6144]{0:T(1024)S(1)}, s32[6144]{0:T(1024)}, u32[]{:S(2)}) copy-start(s32[6144]{0:T(1024)} %param.11) | copy-start | bytes 73732
Sparse Core Ops, SparseCore 0:
  98.7 53.1 all-reduce.3
